TPU v7x, 256 devices: a whole 4x4x8 slice. The times are simulated.
256 devices in a mesh: seq: 32 (over y, x, core), exp: 8 (over z).
Axes of the slice: x: 4, y: 4, z: 8, core: 2. Of those that a mesh axis runs over, the one named last changes fastest.
Arguments:
- queries: bfloat16 [4096, 7168], P('seq', 'exp'), may hold values from -8 to 8
- keys: bfloat16 [4096, 7168], P('seq', 'exp'), may hold values from -8 to 8
- values: bfloat16 [4096, 7168], P('seq', 'exp'), may hold values from -34 to 34
- branch_gates: float32 [4096, 2, 56], P('seq', None, 'exp'), may hold values from 0.1 to 1
- block_choice: int32 [64, 8], P('seq'), may hold values from 0 to 14, as said below
- norm_gain: float32 [7168], P('exp'), may hold values from 0.5 to 1.5
- expert_ids: int32 [4096, 8], P('seq'), may hold values from 0 to 31, all different within a row; in each aligned block of 128 rows (0 to 127, 128 to 255, ...) at most 40 rows name the same one
- route_scores: float32 [4096, 8], P('seq'), may hold values from 0.05 to 1
- w_gate_up: bfloat16 [32, 7168, 2, 1536], P('seq', 'exp'), may hold values from -0.0625 to 0.0625
- w_down: bfloat16 [32, 1536, 7168], P('seq', None, 'exp'), may hold values from -0.15625 to 0.15625
Outputs:
- mixed: bfloat16 [4096, 7168], P('seq', 'exp')
Inputs may be any that keep to these rules, and one draw needn't show every extreme that they name: `block_choice`: each row holds offset 0 and 7 other distinct offsets. `expert_ids`: each row names 8 different experts; within each aligned block of 128 rows (the rows of one index of seq) no expert is named more than 40 times, and that many is reached.
All inputs are finite; a program needn't handle non-finite values.
Results may differ from a plain program's by a relative error of at most 0.029.
Values may be sent and summed in bfloat16 or wider, within the bound.
No kernel may reach another device: no remote copies, remote signals or barrier semaphores. Data moves between devices by JAX's collectives and lax.ppermute only.
A program may use at most 128 MiB of HBM per device.

v0:
```python
import jax
import jax.numpy as jnp
from jax import lax
from jax.sharding import PartitionSpec as P

HD = 128
D = 7168
BLOCK = 64
WINDOW = 15
EPSILON = 1e-06
ROUTE_SCALE = 2.5
MASKED_SCORE = -1e30


def copy_for_each(shard, axis):
    copies = jnp.broadcast_to(shard, (lax.axis_size(axis), *shard.shape))
    return lax.all_to_all(copies, axis, split_axis=0, concat_axis=0, tiled=True)


def joined_along(parts, dim):
    parts = jnp.moveaxis(parts, 0, dim)
    shape = parts.shape
    return parts.reshape(*shape[:dim], shape[dim] * shape[dim + 1], *shape[dim + 2 :])


def collect(shard, axis, dim):
    parts = copy_for_each(shard, axis)
    return joined_along(parts, dim)


def passed_along(shard, axis, by):
    peers = lax.axis_size(axis)
    pairs = [(i, i + by) for i in range(peers) if 0 <= i + by < peers]
    return lax.ppermute(shard, axis, pairs)


def local(
    queries,
    keys,
    values,
    branch_gates,
    block_choice,
    norm_gain,
    expert_ids,
    route_scores,
    w_gate_up,
    w_down,
):
    tokens_here = queries.shape[0]
    features = queries.shape[1]
    heads_here = features // HD
    blocks_here = tokens_here // BLOCK
    device_row = lax.axis_index("seq")
    seq_devices = lax.axis_size("seq")
    score_scale = HD ** (-0.5)
    query_heads = queries.reshape(tokens_here, heads_here, HD)
    positions = jnp.arange(tokens_here, dtype=jnp.int32)
    query_block = device_row * blocks_here + positions // BLOCK
    query_pos = device_row * tokens_here + positions
    chosen = jnp.repeat(block_choice, BLOCK, axis=0)
    local_kv = jnp.stack([keys, values])
    pooled = jnp.mean(
        local_kv.astype(jnp.float32).reshape(2, blocks_here, BLOCK, features), axis=2
    ).astype(jnp.bfloat16)
    everyone = collect(pooled, "seq", 1)
    all_blocks = everyone.shape[1]
    pooled_keys = everyone[0].reshape(all_blocks, heads_here, HD)
    pooled_values = everyone[1].reshape(all_blocks, heads_here, HD)
    scores = (
        jnp.einsum("qhd,chd->hqc", query_heads, pooled_keys, preferred_element_type=jnp.float32)
        * score_scale
    )
    earlier = jnp.arange(all_blocks, dtype=jnp.int32)[None, :] < query_block[:, None]
    masked = jnp.where(earlier[None], scores, MASKED_SCORE)
    row_max = jnp.max(masked, axis=2, keepdims=True)
    row_max = jnp.where(row_max > 0.5 * MASKED_SCORE, row_max, 0.0)
    weights = jnp.where(earlier[None], jnp.exp(scores - row_max), 0.0)
    weight_sum = jnp.sum(weights, axis=2)
    coarse_out = jnp.einsum(
        "hqc,chd->hqd",
        weights.astype(jnp.bfloat16),
        pooled_values,
        preferred_element_type=jnp.float32,
    )
    coarse_out = coarse_out / jnp.maximum(weight_sum, 1.0)[..., None]

    def attend(carried, kv_piece, first_block):
        running_max, denominator, numerator = carried
        key_count = kv_piece.shape[1]
        key_heads = kv_piece[0].reshape(key_count, heads_here, HD)
        value_heads = kv_piece[1].reshape(key_count, heads_here, HD)
        key_offsets = jnp.arange(key_count, dtype=jnp.int32)
        key_block = first_block + key_offsets // BLOCK
        key_pos = first_block * BLOCK + key_offsets
        block_gap = query_block[:, None] - key_block[None, :]
        picked = jnp.any(chosen[:, :, None] == block_gap[:, None, :], axis=1)
        allowed = picked & (key_block >= 0)[None, :] & (key_pos[None, :] <= query_pos[:, None])
        piece_scores = (
            jnp.einsum("qhd,khd->hqk", query_heads, key_heads, preferred_element_type=jnp.float32)
            * score_scale
        )
        piece_masked = jnp.where(allowed[None], piece_scores, MASKED_SCORE)
        updated_max = jnp.maximum(running_max, jnp.max(piece_masked, axis=2))
        piece_weights = jnp.where(
            allowed[None], jnp.exp(piece_scores - updated_max[..., None]), 0.0
        )
        rescale = jnp.exp(running_max - updated_max)
        denominator = denominator * rescale + jnp.sum(piece_weights, axis=2)
        numerator = numerator * rescale[..., None] + jnp.einsum(
            "hqk,khd->hqd",
            piece_weights.astype(jnp.bfloat16),
            value_heads,
            preferred_element_type=jnp.float32,
        )
        return (updated_max, denominator, numerator)

    carried = (
        jnp.full((heads_here, tokens_here), MASKED_SCORE, jnp.float32),
        jnp.zeros((heads_here, tokens_here), jnp.float32),
        jnp.zeros((heads_here, tokens_here, HD), jnp.float32),
    )
    carried = attend(carried, local_kv, device_row * blocks_here)
    reach_devices = min(seq_devices - 1, (WINDOW - 2) // blocks_here + 1)
    gathered = local_kv
    stride = 1
    while stride <= reach_devices:
        incoming = passed_along(gathered, "seq", stride)
        carried = attend(carried, incoming, (device_row - 2 * stride + 1) * blocks_here)
        gathered = jnp.concatenate([incoming, gathered], axis=1)
        stride = stride * 2
    fine_out = carried[2] / carried[1][..., None]
    mixed_heads = (
        jnp.transpose(branch_gates[:, 0, :])[..., None] * coarse_out
        + jnp.transpose(branch_gates[:, 1, :])[..., None] * fine_out
    )
    hidden_state = (
        jnp.transpose(mixed_heads, (1, 0, 2)).reshape(tokens_here, features).astype(jnp.bfloat16)
    )
    routes_per = expert_ids.shape[1]
    capacity = 5 * tokens_here * routes_per // (4 * seq_devices)
    flat_ids = expert_ids.reshape(-1)
    onehot = (flat_ids[:, None] == jnp.arange(seq_devices, dtype=jnp.int32)[None, :]).astype(
        jnp.int32
    )
    slot_index = jnp.sum((jnp.cumsum(onehot, axis=0) - 1) * onehot, axis=1)
    destination = flat_ids * capacity + slot_index
    rows_of = jnp.arange(tokens_here * routes_per, dtype=jnp.int32) // routes_per
    outgoing = (
        jnp.zeros((seq_devices * capacity, features), jnp.bfloat16)
        .at[destination]
        .set(hidden_state[rows_of])
    )
    outgoing = outgoing.reshape(seq_devices, capacity, features)
    arrived = lax.all_to_all(outgoing, "seq", split_axis=0, concat_axis=0, tiled=True)
    sources = arrived.shape[0]
    slots = arrived.shape[1]
    wide_rows = arrived.reshape(sources * slots, features).astype(jnp.float32)
    squares = jnp.sum(wide_rows * wide_rows, axis=1)
    normed = (wide_rows * norm_gain).astype(jnp.bfloat16)
    partials = jnp.einsum("rd,dgh->rgh", normed, w_gate_up[0], preferred_element_type=jnp.float32)
    spread = jnp.broadcast_to(squares[:, None], (squares.shape[0], lax.axis_size("exp")))
    summed = lax.psum_scatter(
        partials.astype(jnp.bfloat16), "exp", scatter_dimension=2, tiled=True
    ).astype(jnp.float32)
    square_share = lax.psum_scatter(
        spread.astype(jnp.bfloat16), "exp", scatter_dimension=1, tiled=True
    ).astype(jnp.float32)
    row_scale = lax.rsqrt(square_share[:, 0] / D + EPSILON)[:, None]
    activated = (jax.nn.silu(summed[:, 0] * row_scale) * (summed[:, 1] * row_scale)).astype(
        jnp.bfloat16
    )
    down_rows = w_down[0]
    result = jnp.dot(
        lax.all_gather(activated, "exp", axis=1, tiled=True),
        down_rows,
        preferred_element_type=jnp.float32,
    )
    results_here = result.astype(jnp.bfloat16).reshape(sources, slots, features)
    returned = lax.all_to_all(results_here, "seq", split_axis=0, concat_axis=0, tiled=True)
    flattened = returned.reshape(seq_devices * capacity, features)
    picked_rows = flattened[destination].reshape(tokens_here, routes_per, features)
    route_weight = ROUTE_SCALE * route_scores / jnp.sum(route_scores, axis=1, keepdims=True)
    routed = jnp.einsum("tk,tkd->td", route_weight, picked_rows.astype(jnp.float32))
    return (hidden_state.astype(jnp.float32) + routed).astype(jnp.bfloat16)


def solution(mesh):
    placed = (
        P("seq", "exp"),
        P("seq", "exp"),
        P("seq", "exp"),
        P("seq", None, "exp"),
        P("seq", None),
        P("exp"),
        P("seq", None),
        P("seq", None),
        P("seq", "exp", None, None),
        P("seq", None, "exp"),
    )
    return jax.shard_map(
        local, mesh=mesh, in_specs=placed, out_specs=P("seq", "exp"), check_vma=False
    )
```

profile of v0, /device:TPU:1, one launch (start us, length us, event | category | flops | bytes accessed | tf_op | source)
XLA Modules:
  0.0 424.2 jit_solution(7948450174983795036)
XLA Ops:
  9.8 4.5 %collective-permute-start = (bf16[2,128,896]{1,2,0:T(8,128)(2,1)}, bf16[2,128,896]{1,2,0:T(8,128)(2,1)}, u32[]{:S(2)}, u32[]{:S(2)}) collective-permute-start(bf16[2,128,896]{1,2,0:T(8,128)(2,1)} %pad_maximum_fusion), channel_id=1, source_target_pairs={{0,8},{8,16},{16,24},{24,32},{32,40},{40,48},{48,56},{56,64},{64,7... | collective-permute-start | bytes 1376264 | tf_op jit(solution)/shard_map/ppermute | solution.py:34
  16.1 7.0 %all-to-all-start = ((bf16[32,2,2,896]{3,2,1,0:T(2,128)(2,1)}), bf16[32,2,2,896]{3,2,1,0:T(2,128)(2,1)}, u32[]{:S(2)}, u32[]{:S(2)}) async-start(bf16[32,2,2,896]{3,2,1,0:T(2,128)(2,1)} %broadcast_in_dim.167), calls=%async_computation | async-start | bytes 458752 | tf_op jit(solution)/shard_map/all_to_all | solution.py:17
  30.8 15.6 %reduce-window.6 = s32[32,8,128]{2,1,0:T(8,128)S(1)} reduce-window(s32[32,8,128]{2,1,0:T(8,128)} %fusion.62, s32[]{:T(128)} %constant.123.clone.1), window={size=1x1x128 pad=0_0x0_0x127_0}, to_apply=%region_16.17 | reduce-window | flops 4161536 | bytes 262148 | tf_op jit(solution)/shard_map/reduce-window
  68.8 2.0 maximum_maximum_fusion.1
  70.8 4.2 collective-permute-start.1
  75.6 1.6 select_reduce_fusion.2
  77.8 1.8 fusion.97
  79.7 1.6 reshape_squeeze.24
  81.3 12.4 %collective-permute-done.1 = bf16[2,256,896]{1,2,0:T(8,128)(2,1)} collective-permute-done((bf16[2,256,896]{1,2,0:T(8,128)(2,1)}, bf16[2,256,896]{1,2,0:T(8,128)(2,1)}, u32[]{:S(2)}, u32[]{:S(2)}) %collective-permute-start.1) | collective-permute-done | bytes 917536 | tf_op jit(solution)/shard_map/ppermute | solution.py:34
  93.7 2.7 maximum_maximum_fusion
  96.4 6.8 %collective-permute-start.2 = (bf16[2,512,896]{1,2,0:T(8,128)(2,1)}, bf16[2,512,896]{1,2,0:T(8,128)(2,1)}, u32[]{:S(2)}, u32[]{:S(2)}) collective-permute-start(bf16[2,512,896]{1,2,0:T(8,128)(2,1)} %maximum_maximum_fusion), channel_id=1, source_target_pairs={{0,32},{8,40},{16,48},{24,56},{32,64},{40,72},{48,80},{56,88},{64,... | collective-permute-start | bytes 5505032 | tf_op jit(solution)/shard_map/ppermute | solution.py:34
  104.1 1.6 reshape_squeeze.25
  111.3 29.2 %collective-permute-done.2 = bf16[2,512,896]{1,2,0:T(8,128)(2,1)} collective-permute-done((bf16[2,512,896]{1,2,0:T(8,128)(2,1)}, bf16[2,512,896]{1,2,0:T(8,128)(2,1)}, u32[]{:S(2)}, u32[]{:S(2)}) %collective-permute-start.2) | collective-permute-done | bytes 1835040 | tf_op jit(solution)/shard_map/ppermute | solution.py:34
  145.7 13.9 %scatter_custom_fusion = bf16[1280,896]{1,0:T(8,128)(2,1)} fusion(s32[1024]{0:T(1024)S(1)} %bitcast.247, bf16[128,896]{1,0:T(8,128)(2,1)S(1)} %copy.118, s32[1024]{0:T(1024)} %broadcast_clamp_fusion.1, bf16[]{:T(256)} %constant.138.clone.1), kind=kCustom, calls=%fused_computation.20 | custom fusion | bytes 2294272 | tf_op jit(solution)/shard_map/scatter | solution.py:151
  159.5 41.4 %all_to_all.15 = bf16[32,40,896]{2,1,0:T(8,128)(2,1)S(1)} all-to-all(bf16[32,40,896]{2,1,0:T(8,128)(2,1)} %bitcast.216), channel_id=1, replica_groups=mesh['seq'=32,'exp'=8] {'seq'}, dimensions={0} | all-to-all | bytes 4587520 | tf_op jit(solution)/shard_map/all_to_all | solution.py:154
  201.7 16.0 %convolution_convert_fusion = bf16[1280,2,1536]{0,2,1:T(8,128)(2,1)} fusion(bf16[1280,896,1]{1,0,2:T(8,128)(2,1)S(1)} %bitcast.232, bf16[896,2,1536]{2,1,0:T(2,128)(2,1)} %bitcast.252), kind=kOutput, calls=%fused_computation.3 | convolution fusion | flops 7050362880 | bytes 15663104 | tf_op jit(solution)/shard_map/rd,dgh->rgh/dot_general | solution.py:160
  219.0 29.2 %all-reduce = bf16[1280,8]{0,1:T(8,128)(2,1)S(1)} all-reduce(bf16[1280,8]{0,1:T(8,128)(2,1)S(1)} %broadcast_in_dim.186), channel_id=3, replica_groups=mesh['seq'=32,'exp'=8] {'exp'}, use_global_device_ids=true, to_apply=%region_22.23.clone | all-reduce | flops 10240 | bytes 40960
  248.8 58.5 %reduce-scatter.2.cloned.1.call-done = bf16[1280,2,192]{0,2,1:T(8,128)(2,1)} async-done(((bf16[1280,2,1536]{0,2,1:T(8,128)(2,1)}), bf16[1280,2,192]{0,2,1:T(8,128)(2,1)}) %reduce-scatter.2.cloned.1.call-update) | async-done | bytes 983056 | tf_op jit(solution)/shard_map/reduce_scatter | solution.py:162
  309.8 50.7 %all-gather.2.cloned.1.call-done = bf16[1280,1536]{0,1:T(8,128)(2,1)} async-done(((bf16[1280,192]{0,1:T(8,128)(2,1)}), bf16[1280,1536]{0,1:T(8,128)(2,1)}) %all-gather.2.cloned.1.call-update) | async-done | bytes 3932176 | tf_op jit(solution)/shard_map/all_gather | solution.py:174
  360.4 7.6 %convolution_convert_fusion.1 = bf16[1280,896]{1,0:T(8,128)(2,1)} fusion(bf16[1280,1536]{0,1:T(8,128)(2,1)} %all-gather.2.cloned.1.call-done, bf16[1,1536,896]{2,1,0:T(8,128)(2,1)S(1)} %copy-done), kind=kOutput, calls=%fused_computation.9 | convolution fusion | flops 3524362240 | bytes 8978432 | tf_op jit(solution)/shard_map/dot_general | solution.py:173
  368.0 7.9 %all-to-all-start.2 = ((bf16[32,40,896]{2,1,0:T(8,128)(2,1)}), bf16[32,40,896]{2,1,0:T(8,128)(2,1)}, u32[]{:S(2)}, u32[]{:S(2)}) async-start(bf16[32,40,896]{2,1,0:T(8,128)(2,1)} %bitcast.231), calls=%async_computation.3 | async-start | bytes 4587520 | tf_op jit(solution)/shard_map/all_to_all | solution.py:179
  376.1 30.6 %all-to-all-done.2 = bf16[32,40,896]{2,1,0:T(8,128)(2,1)} async-done(((bf16[32,40,896]{2,1,0:T(8,128)(2,1)}), bf16[32,40,896]{2,1,0:T(8,128)(2,1)}, u32[]{:S(2)}, u32[]{:S(2)}) %all-to-all-start.2) | async-done | bytes 2293792 | tf_op jit(solution)/shard_map/all_to_all | solution.py:179
  406.7 7.7 %gather_fusion = bf16[1024,896]{1,0:T(8,128)(2,1)} fusion(bf16[1280,896]{1,0:T(8,128)(2,1)} %bitcast.50, s32[1024]{0:T(1024)S(1)} %broadcast_clamp_fusion), kind=kCustom, calls=%fused_computation.1 | custom fusion | bytes 3674112 | tf_op jit(solution)/shard_map/gather | solution.py:181
  414.4 2.2 fusion.4
  (127 shorter events, 53.8 us)
Async XLA Ops:
  6.5 353.9 %copy-start = (bf16[1,1536,896]{2,1,0:T(8,128)(2,1)S(1)}, bf16[1,1536,896]{2,1,0:T(8,128)(2,1)}, u32[]{:S(2)}) copy-start(bf16[1,1536,896]{2,1,0:T(8,128)(2,1)} %param.19) | copy-start | bytes 8257540
  6.5 7.7 %copy-start.2 = (bf16[128,896]{1,0:T(8,128)(2,1)S(1)}, bf16[128,896]{1,0:T(8,128)(2,1)}, u32[]{:S(2)}) copy-start(bf16[128,896]{1,0:T(8,128)(2,1)} %param.12) | copy-start | bytes 688132
  6.5 19.8 %copy-start.16 = (s32[2,8]{1,0:T(2,128)S(1)}, s32[2,8]{1,0:T(2,128)}, u32[]{:S(2)}) copy-start(s32[2,8]{1,0:T(2,128)} %param.14) | copy-start | bytes 196
  7.8 21.5 %copy-start.13 = (f32[128,2,7]{0,1,2:T(2,128)S(1)}, f32[128,2,7]{0,1,2:T(2,128)}, u32[]{:S(2)}) copy-start(f32[128,2,7]{0,1,2:T(2,128)} %param.13) | copy-start | bytes 21508
  7.8 22.1 %copy-start.10 = (s32[128,8]{0,1:T(8,128)S(1)}, s32[128,8]{0,1:T(8,128)}, u32[]{:S(2)}) copy-start(s32[128,8]{0,1:T(8,128)} %param.16) | copy-start | bytes 12292
  9.8 59.0 %collective-permute-start = (bf16[2,128,896]{1,2,0:T(8,128)(2,1)}, bf16[2,128,896]{1,2,0:T(8,128)(2,1)}, u32[]{:S(2)}, u32[]{:S(2)}) collective-permute-start(bf16[2,128,896]{1,2,0:T(8,128)(2,1)} %pad_maximum_fusion), channel_id=1, source_target_pairs={{0,8},{8,16},{16,24},{24,32},{32,40},{40,48},{48,56},{56,64},{64,7... | collective-permute-start | bytes 1376264 | tf_op jit(solution)/shard_map/ppermute | solution.py:34
  16.1 61.7 %all-to-all-start = ((bf16[32,2,2,896]{3,2,1,0:T(2,128)(2,1)}), bf16[32,2,2,896]{3,2,1,0:T(2,128)(2,1)}, u32[]{:S(2)}, u32[]{:S(2)}) async-start(bf16[32,2,2,896]{3,2,1,0:T(2,128)(2,1)} %broadcast_in_dim.167), calls=%async_computation | async-start | bytes 458752 | tf_op jit(solution)/shard_map/all_to_all | solution.py:17
  23.1 284.2 %reduce-scatter.2.cloned.1.call-start = ((), (), s32[]{:S(2)}) async-start(), calls=%async_computation.4 | async-start | bytes 8847360 | tf_op jit(solution)/shard_map/reduce_scatter | solution.py:162
  23.2 3.1 copy-start.8
  66.5 8.5 %copy-start.9 = (s32[128]{0:T(128)S(1)}, s32[128]{0:T(128)}, u32[]{:S(2)}) copy-start(s32[128]{0:T(128)} %copy-done.8) | copy-start | bytes 1540
  66.5 9.1 %copy-start.4 = (pred[128,128]{0,1:T(8,128)(4,1)S(1)}, pred[128,128]{0,1:T(8,128)(4,1)}, u32[]{:S(2)}) copy-start(pred[128,128]{0,1:T(8,128)(4,1)} %copy.97) | copy-start | bytes 49156
  70.8 22.9 %collective-permute-start.1 = (bf16[2,256,896]{1,2,0:T(8,128)(2,1)}, bf16[2,256,896]{1,2,0:T(8,128)(2,1)}, u32[]{:S(2)}, u32[]{:S(2)}) collective-permute-start(bf16[2,256,896]{1,2,0:T(8,128)(2,1)} %maximum_maximum_fusion.1), channel_id=1, source_target_pairs={{0,16},{8,24},{16,32},{24,40},{32,48},{40,56},{48,64},{56,72},{64,... | collective-permute-start | bytes 2752520 | tf_op jit(solution)/shard_map/ppermute | solution.py:34
  81.3 21.9 %copy-start.3 = (bf16[64,7,128]{2,1,0:T(8,128)(2,1)S(1)}, bf16[64,7,128]{2,1,0:T(8,128)(2,1)}, u32[]{:S(2)}) copy-start(bf16[64,7,128]{2,1,0:T(8,128)(2,1)} %reshape_squeeze.24) | copy-start | bytes 344068
  81.3 21.9 %copy-start.6 = (pred[128,64]{0,1:T(8,128)(4,1)S(1)}, pred[128,64]{0,1:T(8,128)(4,1)}, u32[]{:S(2)}) copy-start(pred[128,64]{0,1:T(8,128)(4,1)} %iota_compare_fusion.2) | copy-start | bytes 24580
  96.4 44.0 %collective-permute-start.2 = (bf16[2,512,896]{1,2,0:T(8,128)(2,1)}, bf16[2,512,896]{1,2,0:T(8,128)(2,1)}, u32[]{:S(2)}, u32[]{:S(2)}) collective-permute-start(bf16[2,512,896]{1,2,0:T(8,128)(2,1)} %maximum_maximum_fusion), channel_id=1, source_target_pairs={{0,32},{8,40},{16,48},{24,56},{32,64},{40,72},{48,80},{56,88},{64,... | collective-permute-start | bytes 5505032 | tf_op jit(solution)/shard_map/ppermute | solution.py:34
  142.0 0.7 copy-start.7
  142.6 1.0 copy-start.1
  142.6 1.0 copy-start.5
  144.2 0.7 copy-start.14
  144.9 0.8 copy-start.11
  159.5 41.4 %copy-start.15 = (f32[896]{0:T(1024)S(1)}, f32[896]{0:T(1024)}, u32[]{:S(2)}) copy-start(f32[896]{0:T(1024)} %param.15) | copy-start | bytes 10756
  217.6 142.8 %all-gather.2.cloned.1.call-start = ((), (), s32[]{:S(2)}) async-start(), calls=%async_computation.5 | async-start | bytes 4423680 | tf_op jit(solution)/shard_map/all_gather | solution.py:174
  368.0 7.9 %copy-start.12 = (f32[128,8]{0,1:T(8,128)S(1)}, f32[128,8]{0,1:T(8,128)}, u32[]{:S(2)}) copy-start(f32[128,8]{0,1:T(8,128)} %param.17) | copy-start | bytes 12292
  368.0 38.7 %all-to-all-start.2 = ((bf16[32,40,896]{2,1,0:T(8,128)(2,1)}), bf16[32,40,896]{2,1,0:T(8,128)(2,1)}, u32[]{:S(2)}, u32[]{:S(2)}) async-start(bf16[32,40,896]{2,1,0:T(8,128)(2,1)} %bitcast.231), calls=%async_computation.3 | async-start | bytes 4587520 | tf_op jit(solution)/shard_map/all_to_all | solution.py:179
  (1 other events, 0.7 us)
Sparse Core Ops, SparseCore 0:
  217.8 89.5 reduce-scatter.1
  309.9 50.5 all-gather.1
where the time goes:
time: 427 us; the launch traced here: 424 us
  waiting for transfers between devices  181 us (42%)
  blocking collectives  70.6 us (17%)
  local copies, waits for them, and re-layouts  49.8 us (12%)
  other arithmetic  46.3 us (11%)
  matrix products  31.9 us (7%)
  starting transfers between devices  30.4 us (7%)
  between operations  13.8 us (3%)
    reduce_scatter x1, waiting for transfers between devices, local(): lax.psum_scatter(partials.astype(jnp.bfloat16), 'exp', scatter_dimension=...  58.5 us
    all_gather x1, waiting for transfers between devices, local(): lax.all_gather(activated, 'exp', axis=1, tiled=True)  50.7 us
    ppermute x3, waiting for transfers between devices, passed_along(): return lax.ppermute(shard, axis, pairs)  41.5 us
    all_to_all x1, blocking collectives, local(): lax.all_to_all(outgoing, 'seq', split_axis=0, concat_axis=0, tiled=True)  41.4 us
    all_to_all x1, waiting for transfers between devices, local(): lax.all_to_all(results_here, 'seq', split_axis=0, concat_axis=0, tiled=True)  30.6 us
    unnamed x1, blocking collectives  29.2 us
    dot_general x1, matrix products, local(): jnp.einsum('rd,dgh->rgh', normed, w_gate_up[0], preferred_element_type=jn...  16 us
    another operation x2, other arithmetic  15.6 us
  transfers between devices with their start and end apart: 7, of which 5 were waited for; matrix products, arithmetic and copies ran while one was open for 15% of the time, Pallas kernels for 0%

commit v1 on v0

--- a/solution.py
+++ b/solution.py
@@ -10,6 +10,16 @@
 EPSILON = 1e-06
 ROUTE_SCALE = 2.5
 MASKED_SCORE = -1e30
+
+
+def open_the_unit(inner_x, named_axis):
+    pages = []
+    for _ in range(lax.axis_size(named_axis)):
+        pages.append(inner_x)
+    d_next = jnp.stack(pages, axis=0)
+    side_arr = lax.all_to_all(d_next, named_axis, 0, 0)
+    part_next = jnp.concatenate(side_arr, 1)
+    return part_next
 
 
 def copy_for_each(shard, axis):
@@ -170,11 +180,7 @@
         jnp.bfloat16
     )
     down_rows = w_down[0]
-    result = jnp.dot(
-        lax.all_gather(activated, "exp", axis=1, tiled=True),
-        down_rows,
-        preferred_element_type=jnp.float32,
-    )
+    result = jnp.dot(open_the_unit(activated, "exp"), down_rows, preferred_element_type=jnp.float32)
     results_here = result.astype(jnp.bfloat16).reshape(sources, slots, features)
     returned = lax.all_to_all(results_here, "seq", split_axis=0, concat_axis=0, tiled=True)
     flattened = returned.reshape(seq_devices * capacity, features)

time: 427 us -> 468 us (1.096)
  blocking collectives: 70.6 us -> 163 us
  waiting for transfers between devices: 181 us -> 131 us
    all_to_all x0 -> x1, blocking collectives: none -> 92.6 us  [open_the_unit(): side_arr = lax.all_to_all(d_next, named_axis, 0, 0)]
    all_gather x1 -> x0, waiting for transfers between devices: 50.7 us -> none  [local(): lax.all_gather(activated, 'exp', axis=1, tiled=True)]
  transfers between devices with their start and end apart: 7 -> 6, of which waited for: 5 -> 4; matrix products, arithmetic and copies ran while one was open for 15% -> 14% of each run, Pallas kernels for 0% -> 0%
where the time goes in v1:
time: 468 us; the launch traced here: 465 us
  blocking collectives  163 us (35%)
  waiting for transfers between devices  131 us (28%)
  local copies, waits for them, and re-layouts  50.2 us (11%)
  other arithmetic  45.5 us (10%)
  starting transfers between devices  31.9 us (7%)
  matrix products  29.8 us (6%)
  between operations  13.8 us (3%)
    all_to_all x1, blocking collectives, open_the_unit(): side_arr = lax.all_to_all(d_next, named_axis, 0, 0)  92.6 us
    reduce_scatter x1, waiting for transfers between devices, local(): lax.psum_scatter(partials.astype(jnp.bfloat16), 'exp', scatter_dimension=...  58.5 us
    ppermute x3, waiting for transfers between devices, passed_along(): return lax.ppermute(shard, axis, pairs)  41.5 us
    all_to_all x1, blocking collectives, local(): lax.all_to_all(outgoing, 'seq', split_axis=0, concat_axis=0, tiled=True)  41.4 us
    all_to_all x1, waiting for transfers between devices, local(): lax.all_to_all(results_here, 'seq', split_axis=0, concat_axis=0, tiled=True)  30.6 us
    unnamed x1, blocking collectives  29.2 us
    dot_general x1, matrix products, local(): jnp.einsum('rd,dgh->rgh', normed, w_gate_up[0], preferred_element_type=jn...  16 us
    another operation x2, other arithmetic  15.6 us
  transfers between devices with their start and end apart: 6, of which 4 were waited for; matrix products, arithmetic and copies ran while one was open for 14% of the time, Pallas kernels for 0%

profile of v1, /device:TPU:1, one launch (start us, length us, event | category | flops | bytes accessed | tf_op | source)
XLA Modules:
  0.0 465.1 jit_solution(17120051237919265335)
XLA Ops:
  9.8 4.5 collective-permute-start
  16.1 7.0 %all-to-all-start = ((bf16[32,2,2,896]{3,2,1,0:T(2,128)(2,1)}), bf16[32,2,2,896]{3,2,1,0:T(2,128)(2,1)}, u32[]{:S(2)}, u32[]{:S(2)}) async-start(bf16[32,2,2,896]{3,2,1,0:T(2,128)(2,1)} %broadcast_in_dim.167), calls=%async_computation | async-start | bytes 458752 | tf_op jit(solution)/shard_map/all_to_all | solution.py:27
  30.8 15.6 %reduce-window.6 = s32[32,8,128]{2,1,0:T(8,128)S(1)} reduce-window(s32[32,8,128]{2,1,0:T(8,128)} %fusion.62, s32[]{:T(128)} %constant.123.clone.1), window={size=1x1x128 pad=0_0x0_0x127_0}, to_apply=%region_16.17 | reduce-window | flops 4161536 | bytes 262148 | tf_op jit(solution)/shard_map/reduce-window
  68.8 2.0 maximum_maximum_fusion.1
  70.8 4.2 collective-permute-start.1
  75.6 1.6 select_reduce_fusion.2
  77.8 1.8 fusion.97
  79.7 1.6 reshape_squeeze.24
  81.3 12.4 %collective-permute-done.1 = bf16[2,256,896]{1,2,0:T(8,128)(2,1)} collective-permute-done((bf16[2,256,896]{1,2,0:T(8,128)(2,1)}, bf16[2,256,896]{1,2,0:T(8,128)(2,1)}, u32[]{:S(2)}, u32[]{:S(2)}) %collective-permute-start.1) | collective-permute-done | bytes 917536 | tf_op jit(solution)/shard_map/ppermute | solution.py:44
  93.7 2.7 maximum_maximum_fusion
  96.4 6.8 %collective-permute-start.2 = (bf16[2,512,896]{1,2,0:T(8,128)(2,1)}, bf16[2,512,896]{1,2,0:T(8,128)(2,1)}, u32[]{:S(2)}, u32[]{:S(2)}) collective-permute-start(bf16[2,512,896]{1,2,0:T(8,128)(2,1)} %maximum_maximum_fusion), channel_id=1, source_target_pairs={{0,32},{8,40},{16,48},{24,56},{32,64},{40,72},{48,80},{56,88},{64,... | collective-permute-start | bytes 5505032 | tf_op jit(solution)/shard_map/ppermute | solution.py:44
  104.1 1.6 reshape_squeeze.25
  111.3 29.2 %collective-permute-done.2 = bf16[2,512,896]{1,2,0:T(8,128)(2,1)} collective-permute-done((bf16[2,512,896]{1,2,0:T(8,128)(2,1)}, bf16[2,512,896]{1,2,0:T(8,128)(2,1)}, u32[]{:S(2)}, u32[]{:S(2)}) %collective-permute-start.2) | collective-permute-done | bytes 1835040 | tf_op jit(solution)/shard_map/ppermute | solution.py:44
  145.7 13.9 %scatter_custom_fusion = bf16[1280,896]{1,0:T(8,128)(2,1)} fusion(s32[1024]{0:T(1024)S(1)} %bitcast.251, bf16[128,896]{1,0:T(8,128)(2,1)S(1)} %copy.119, s32[1024]{0:T(1024)} %broadcast_clamp_fusion.1, bf16[]{:T(256)} %constant.138.clone.1), kind=kCustom, calls=%fused_computation.20 | custom fusion | bytes 2294272 | tf_op jit(solution)/shard_map/scatter | solution.py:161
  159.5 41.4 %all_to_all.20 = bf16[32,40,896]{2,1,0:T(8,128)(2,1)S(1)} all-to-all(bf16[32,40,896]{2,1,0:T(8,128)(2,1)} %bitcast.219), channel_id=1, replica_groups=mesh['seq'=32,'exp'=8] {'seq'}, dimensions={0} | all-to-all | bytes 4587520 | tf_op jit(solution)/shard_map/all_to_all | solution.py:164
  201.6 16.0 %convolution_convert_fusion = bf16[1280,2,1536]{0,2,1:T(8,128)(2,1)} fusion(bf16[1280,896,1]{1,0,2:T(8,128)(2,1)S(1)} %bitcast.236, bf16[896,2,1536]{2,1,0:T(2,128)(2,1)} %bitcast.256), kind=kOutput, calls=%fused_computation.3 | convolution fusion | flops 7050362880 | bytes 15663104 | tf_op jit(solution)/shard_map/rd,dgh->rgh/dot_general | solution.py:170
  219.0 29.2 %all-reduce = bf16[1280,8]{0,1:T(8,128)(2,1)S(1)} all-reduce(bf16[1280,8]{0,1:T(8,128)(2,1)S(1)} %broadcast_in_dim.186), channel_id=3, replica_groups=mesh['seq'=32,'exp'=8] {'exp'}, use_global_device_ids=true, to_apply=%region_22.23.clone | all-reduce | flops 10240 | bytes 40960
  248.8 58.5 %reduce-scatter.2.cloned.1.call-done = bf16[1280,2,192]{0,2,1:T(8,128)(2,1)} async-done(((bf16[1280,2,1536]{0,2,1:T(8,128)(2,1)}), bf16[1280,2,192]{0,2,1:T(8,128)(2,1)}) %reduce-scatter.2.cloned.1.call-update) | async-done | bytes 983056 | tf_op jit(solution)/shard_map/reduce_scatter | solution.py:172
  309.3 92.6 %all_to_all.21 = bf16[8,1280,192]{1,2,0:T(8,128)(2,1)S(1)} all-to-all(bf16[8,1280,192]{1,2,0:T(8,128)(2,1)S(1)} %stack.32), channel_id=1, replica_groups=mesh['seq'=32,'exp'=8] {'exp'}, dimensions={0} | all-to-all | bytes 7864320 | tf_op jit(solution)/shard_map/all_to_all | solution.py:20
  401.9 5.5 %convolution_convert_fusion.1 = bf16[1280,896]{1,0:T(8,128)(2,1)} fusion(bf16[1280,1536]{0,1:T(8,128)(2,1)S(1)} %bitcast.233, bf16[1,1536,896]{2,1,0:T(8,128)(2,1)S(1)} %copy-done), kind=kOutput, calls=%fused_computation.9 | convolution fusion | flops 3524362240 | bytes 8978432 | tf_op jit(solution)/shard_map/dot_general | solution.py:183
  407.4 9.4 %all-to-all-start.3 = ((bf16[32,40,896]{2,1,0:T(8,128)(2,1)}), bf16[32,40,896]{2,1,0:T(8,128)(2,1)}, u32[]{:S(2)}, u32[]{:S(2)}) async-start(bf16[32,40,896]{2,1,0:T(8,128)(2,1)} %bitcast.235), calls=%async_computation.4 | async-start | bytes 4587520 | tf_op jit(solution)/shard_map/all_to_all | solution.py:185
  417.0 30.6 %all-to-all-done.3 = bf16[32,40,896]{2,1,0:T(8,128)(2,1)} async-done(((bf16[32,40,896]{2,1,0:T(8,128)(2,1)}), bf16[32,40,896]{2,1,0:T(8,128)(2,1)}, u32[]{:S(2)}, u32[]{:S(2)}) %all-to-all-start.3) | async-done | bytes 2293792 | tf_op jit(solution)/shard_map/all_to_all | solution.py:185
  447.7 7.7 %gather_fusion = bf16[1024,896]{1,0:T(8,128)(2,1)} fusion(bf16[1280,896]{1,0:T(8,128)(2,1)} %bitcast.52, s32[1024]{0:T(1024)S(1)} %broadcast_clamp_fusion), kind=kCustom, calls=%fused_computation.1 | custom fusion | bytes 3674112 | tf_op jit(solution)/shard_map/gather | solution.py:187
  455.4 2.2 fusion.4
  (126 shorter events, 53.3 us)
Async XLA Ops:
  6.5 395.4 %copy-start = (bf16[1,1536,896]{2,1,0:T(8,128)(2,1)S(1)}, bf16[1,1536,896]{2,1,0:T(8,128)(2,1)}, u32[]{:S(2)}) copy-start(bf16[1,1536,896]{2,1,0:T(8,128)(2,1)} %param.19) | copy-start | bytes 8257540
  6.5 7.7 %copy-start.2 = (bf16[128,896]{1,0:T(8,128)(2,1)S(1)}, bf16[128,896]{1,0:T(8,128)(2,1)}, u32[]{:S(2)}) copy-start(bf16[128,896]{1,0:T(8,128)(2,1)} %param.12) | copy-start | bytes 688132
  6.5 19.8 %copy-start.16 = (s32[2,8]{1,0:T(2,128)S(1)}, s32[2,8]{1,0:T(2,128)}, u32[]{:S(2)}) copy-start(s32[2,8]{1,0:T(2,128)} %param.14) | copy-start | bytes 196
  7.8 21.5 %copy-start.13 = (f32[128,2,7]{0,1,2:T(2,128)S(1)}, f32[128,2,7]{0,1,2:T(2,128)}, u32[]{:S(2)}) copy-start(f32[128,2,7]{0,1,2:T(2,128)} %param.13) | copy-start | bytes 21508
  7.8 22.1 %copy-start.10 = (s32[128,8]{0,1:T(8,128)S(1)}, s32[128,8]{0,1:T(8,128)}, u32[]{:S(2)}) copy-start(s32[128,8]{0,1:T(8,128)} %param.16) | copy-start | bytes 12292
  9.8 59.0 %collective-permute-start = (bf16[2,128,896]{1,2,0:T(8,128)(2,1)}, bf16[2,128,896]{1,2,0:T(8,128)(2,1)}, u32[]{:S(2)}, u32[]{:S(2)}) collective-permute-start(bf16[2,128,896]{1,2,0:T(8,128)(2,1)} %pad_maximum_fusion), channel_id=1, source_target_pairs={{0,8},{8,16},{16,24},{24,32},{32,40},{40,48},{48,56},{56,64},{64,7... | collective-permute-start | bytes 1376264 | tf_op jit(solution)/shard_map/ppermute | solution.py:44
  16.1 61.7 %all-to-all-start = ((bf16[32,2,2,896]{3,2,1,0:T(2,128)(2,1)}), bf16[32,2,2,896]{3,2,1,0:T(2,128)(2,1)}, u32[]{:S(2)}, u32[]{:S(2)}) async-start(bf16[32,2,2,896]{3,2,1,0:T(2,128)(2,1)} %broadcast_in_dim.167), calls=%async_computation | async-start | bytes 458752 | tf_op jit(solution)/shard_map/all_to_all | solution.py:27
  23.1 284.3 %reduce-scatter.2.cloned.1.call-start = ((), (), s32[]{:S(2)}) async-start(), calls=%async_computation.5 | async-start | bytes 8847360 | tf_op jit(solution)/shard_map/reduce_scatter | solution.py:172
  23.2 3.1 copy-start.8
  66.5 8.5 %copy-start.9 = (s32[128]{0:T(128)S(1)}, s32[128]{0:T(128)}, u32[]{:S(2)}) copy-start(s32[128]{0:T(128)} %copy-done.8) | copy-start | bytes 1540
  66.5 9.1 %copy-start.4 = (pred[128,128]{0,1:T(8,128)(4,1)S(1)}, pred[128,128]{0,1:T(8,128)(4,1)}, u32[]{:S(2)}) copy-start(pred[128,128]{0,1:T(8,128)(4,1)} %copy.98) | copy-start | bytes 49156
  70.8 22.9 %collective-permute-start.1 = (bf16[2,256,896]{1,2,0:T(8,128)(2,1)}, bf16[2,256,896]{1,2,0:T(8,128)(2,1)}, u32[]{:S(2)}, u32[]{:S(2)}) collective-permute-start(bf16[2,256,896]{1,2,0:T(8,128)(2,1)} %maximum_maximum_fusion.1), channel_id=1, source_target_pairs={{0,16},{8,24},{16,32},{24,40},{32,48},{40,56},{48,64},{56,72},{64,... | collective-permute-start | bytes 2752520 | tf_op jit(solution)/shard_map/ppermute | solution.py:44
  81.3 21.9 %copy-start.3 = (bf16[64,7,128]{2,1,0:T(8,128)(2,1)S(1)}, bf16[64,7,128]{2,1,0:T(8,128)(2,1)}, u32[]{:S(2)}) copy-start(bf16[64,7,128]{2,1,0:T(8,128)(2,1)} %reshape_squeeze.24) | copy-start | bytes 344068
  81.3 21.9 %copy-start.6 = (pred[128,64]{0,1:T(8,128)(4,1)S(1)}, pred[128,64]{0,1:T(8,128)(4,1)}, u32[]{:S(2)}) copy-start(pred[128,64]{0,1:T(8,128)(4,1)} %iota_compare_fusion.2) | copy-start | bytes 24580
  96.4 44.0 %collective-permute-start.2 = (bf16[2,512,896]{1,2,0:T(8,128)(2,1)}, bf16[2,512,896]{1,2,0:T(8,128)(2,1)}, u32[]{:S(2)}, u32[]{:S(2)}) collective-permute-start(bf16[2,512,896]{1,2,0:T(8,128)(2,1)} %maximum_maximum_fusion), channel_id=1, source_target_pairs={{0,32},{8,40},{16,48},{24,56},{32,64},{40,72},{48,80},{56,88},{64,... | collective-permute-start | bytes 5505032 | tf_op jit(solution)/shard_map/ppermute | solution.py:44
  142.0 0.7 copy-start.7
  142.6 1.0 copy-start.1
  142.6 1.0 copy-start.5
  144.2 0.7 copy-start.14
  144.9 0.8 copy-start.11
  159.5 41.4 %copy-start.15 = (f32[896]{0:T(1024)S(1)}, f32[896]{0:T(1024)}, u32[]{:S(2)}) copy-start(f32[896]{0:T(1024)} %param.15) | copy-start | bytes 10756
  217.6 0.7 copy-start.17
  407.4 9.4 %copy-start.12 = (f32[128,8]{0,1:T(8,128)S(1)}, f32[128,8]{0,1:T(8,128)}, u32[]{:S(2)}) copy-start(f32[128,8]{0,1:T(8,128)} %param.17) | copy-start | bytes 12292
  407.4 40.3 %all-to-all-start.3 = ((bf16[32,40,896]{2,1,0:T(8,128)(2,1)}), bf16[32,40,896]{2,1,0:T(8,128)(2,1)}, u32[]{:S(2)}, u32[]{:S(2)}) async-start(bf16[32,40,896]{2,1,0:T(8,128)(2,1)} %bitcast.235), calls=%async_computation.4 | async-start | bytes 4587520 | tf_op jit(solution)/shard_map/all_to_all | solution.py:185
Sparse Core Ops, SparseCore 0:
  217.8 89.5 reduce-scatter.1
